TPU v7x, 128 devices: a whole 4x4x4 slice. The times are simulated.
128 devices in a mesh: tile: 16 (over x, z_lo, core), col: 8 (over y, z_hi).
Axes of the slice: x: 4, y: 4, z: 4 (z_hi: 2, z_lo: 2; z = z_hi * 2 + z_lo), core: 2. Of those that a mesh axis runs over, the one named last changes fastest.
Arguments:
- u_velocity: float32 [8192, 4096], P('tile', 'col'), may hold values from -12 to 12
- v_velocity: float32 [8192, 4096], P('tile', 'col'), may hold values from -12 to 12
- ocean_mask: int32 [64, 32], P('tile', 'col'), may hold values from 0 to 1, as said below
- tile_owner: int32 [64, 32], P('tile', 'col'), may hold values from 0 to 15, as said below
- lower_edge_quarter_turns: int32 [16], replicated, may hold values from 0 to 3
Outputs:
- library: float32 [16, 8, 16, 16, 1024], P('tile', 'col')
- gram: float32 [16, 16], replicated
Inputs may be any that keep to these rules, and one draw needn't show every extreme that they name: `ocean_mask`: in every column of devices (4 x 4 tile blocks), at least one device has only ocean tiles. `tile_owner`: among the ocean tiles of one device at most 1 share an owner; the ocean tiles of one column of devices are spread over its 16 owners so that the owners' counts differ by at most one. Land tiles carry an owner that is not used.
All inputs are finite; a program needn't handle non-finite values.
Results may differ from a plain program's by a relative error of at most 0.00014.
Values sent between devices are 32-bit elements; how exact they have to be, the bound alone decides.
No kernel may reach another device: no remote copies, remote signals or barrier semaphores. Data moves between devices by JAX's collectives and lax.ppermute only.
A program may use at most 192 MiB of HBM per device.

v0:
```python
import jax
import jax.numpy as jnp
from jax import lax
from jax.sharding import PartitionSpec as P

PASSES = 8
KAPPA = 0.2


def with_halo(cells, sides, width):
    for axis, dim in sides:
        count = lax.axis_size(axis)
        head = lax.slice_in_dim(cells, 0, width, axis=dim)
        tail = lax.slice_in_dim(cells, cells.shape[dim] - width, cells.shape[dim], axis=dim)
        cells = jnp.concatenate(
            [
                lax.ppermute(tail, axis, [(i, (i + 1) % count) for i in range(count)]),
                cells,
                lax.ppermute(head, axis, [((i + 1) % count, i) for i in range(count)]),
            ],
            axis=dim,
        )
    return cells


def quarter(first, second, turns):
    cosine = jnp.where(turns == 0, 1.0, jnp.where(turns == 2, -1.0, 0.0)).astype(first.dtype)
    sine = jnp.where(turns == 1, 1.0, jnp.where(turns == 3, -1.0, 0.0)).astype(first.dtype)
    return (cosine * first - sine * second, sine * first + cosine * second)


def turn_rims(padded, width, k_top, k_bottom):
    top_u, top_v = quarter(padded[0, :width], padded[1, :width], k_top)
    low_u, low_v = quarter(padded[0, -width:], padded[1, -width:], k_bottom)
    upper = jnp.stack([top_u, top_v])
    lower = jnp.stack([low_u, low_v])
    return jnp.concatenate([upper, padded[:, width:-width], lower], axis=1)


def relax(padded):
    centre = padded[:, 1:-1, 1:-1]
    beside_all = (
        padded[:, :-2, 1:-1] + padded[:, 2:, 1:-1] + padded[:, 1:-1, :-2] + padded[:, 1:-1, 2:]
    )
    return centre + KAPPA * (beside_all - 4.0 * centre)


def derive(padded):
    first = padded[..., 0, :, :]
    second = padded[..., 1, :, :]
    u_part = first[..., 1:-1, 1:-1]
    v_part = second[..., 1:-1, 1:-1]
    u_dx = (first[..., 1:-1, 2:] - first[..., 1:-1, :-2]) * 0.5
    u_dy = (first[..., 2:, 1:-1] - first[..., :-2, 1:-1]) * 0.5
    v_dx = (second[..., 1:-1, 2:] - second[..., 1:-1, :-2]) * 0.5
    v_dy = (second[..., 2:, 1:-1] - second[..., :-2, 1:-1]) * 0.5
    return jnp.stack([u_part, v_part, v_dx - u_dy, u_dy + v_dx, u_dx - v_dy], axis=-3)


def make_terms(base):
    u_part = base[..., 0, :]
    v_part = base[..., 1, :]
    vort = base[..., 2, :]
    strain = base[..., 3, :]
    stretch = base[..., 4, :]
    listed = [
        u_part,
        v_part,
        vort,
        strain,
        stretch,
        vort * vort,
        vort * strain,
        vort * stretch,
        strain * strain,
        stretch * stretch,
        strain * stretch,
        u_part * vort,
        v_part * vort,
        u_part * strain,
        v_part * stretch,
        u_part * v_part,
    ]
    return jnp.stack(listed, axis=-2)


def to_tiles(field, grid_x, grid_y, side):
    leading = field.shape[:-2]
    shaped = field.reshape(leading + (grid_x, side, grid_y, side))
    shaped = jnp.swapaxes(shaped, -3, -2)
    return shaped.reshape(leading + (grid_x * grid_y, side * side))


def per_device(u_velocity, v_velocity, ocean_mask, tile_owner, lower_edge_quarter_turns):
    rows_tile = lax.axis_size("tile")
    here = lax.axis_index("tile")
    k_top = lower_edge_quarter_turns[here]
    k_bottom = (4 - lower_edge_quarter_turns[(here + 1) % rows_tile]) % 4
    field = jnp.stack([u_velocity, v_velocity])
    for step in range(PASSES):
        padded = with_halo(field, (("tile", 1), ("col", 2)), 1)
        field = relax(turn_rims(padded, 1, k_top, k_bottom))
    fine_rows, fine_cols = u_velocity.shape
    coarse = field.reshape(2, fine_rows // 4, 4, fine_cols // 4, 4).mean(axis=(2, 4))
    coarse_pad = with_halo(coarse, (("tile", 1), ("col", 2)), 1)
    coarse_pad = turn_rims(coarse_pad, 1, k_top, k_bottom)
    grid_x, grid_y = ocean_mask.shape
    side = coarse.shape[1] // grid_x
    starting_tile_set = jnp.swapaxes(to_tiles(derive(coarse_pad), grid_x, grid_y, side), 0, 1)
    live = ocean_mask.reshape(-1) == 1
    owners = tile_owner.reshape(-1)
    tiles = live.shape[0]
    slots = tiles // rows_tile
    local = jnp.arange(tiles, dtype=jnp.int32)
    same = (owners[:, None] == owners[None, :]) & live[None, :] & (local[None, :] < local[:, None])
    slot = jnp.sum(same.astype(jnp.int32), axis=1)
    target = jnp.arange(rows_tile * slots, dtype=jnp.int32)
    chosen_terms = (
        live[None, :]
        & (owners[None, :] == target[:, None] // slots)
        & (slot[None, :] == target[:, None] % slots)
    ).astype(jnp.float32)
    library = make_terms(
        lax.all_to_all(
            jnp.einsum(
                "vh,hsd->vsd", chosen_terms, starting_tile_set, precision=lax.Precision.HIGHEST
            ),
            "tile",
            split_axis=0,
            concat_axis=0,
            tiled=True,
        )
    )
    part = jnp.einsum("pnc,pmc->nm", library, library, precision=lax.Precision.HIGHEST)
    gram = lax.psum(part, ("tile", "col")) / (fine_rows // 4 * (fine_cols // 4))
    return (library[None, None], gram)


def solution(mesh):
    in_specs = (P("tile", "col"), P("tile", "col"), P("tile", "col"), P("tile", "col"), P())
    out_specs = (P("tile", "col", None, None, None), P())
    return jax.shard_map(
        per_device, mesh=mesh, in_specs=in_specs, out_specs=out_specs, check_vma=False
    )
```

profile of v0, /device:TPU:1, one launch (start us, length us, event | category | flops | bytes accessed | tf_op | source)
XLA Modules:
  0.0 374.1 jit_solution(4603771623657914441)
XLA Ops:
  1.6 3.1 collective-permute-start
  5.4 2.4 collective-permute-done.1
  8.2 3.5 collective-permute-start.2
  12.0 2.5 collective-permute-start.3
  20.3 1.1 copy-done.12
  21.4 6.4 %fusion.45 = f32[2,512,512]{2,1,0:T(8,128)S(1)} fusion(f32[2,514,1]{2,1,0:T(8,128)} %copy-done.15, f32[2,1,512]{2,1,0:T(1,128)S(1)} %collective-permute-done.1, f32[2,1,512]{2,1,0:T(1,128)S(1)} %collective-permute-done, f32[1,512,512]{2,1,0:T(8,128)S(1)} %bitcast.34, f32[1,512,512]{2,1,0:T(8,128)S(1)} %bitcast.28, f32[2,514,1]{2,1,0:T(8,128)} %copy-done.13, ...), kind=kLoop, calls=%fused_computation.129 | loop fusion | flops 10485760 | bytes 6324288 | tf_op jit(solution)/shard_map/add | solution.py:45
  29.4 1.5 collective-permute-done.5
  32.0 1.3 copy.208
  34.3 4.6 %collective-permute-start.7 = (f32[2,514,1]{1,0,2:T(2,128)S(1)}, f32[2,514,1]{1,0,2:T(2,128)S(1)}, u32[]{:S(2)}, u32[]{:S(2)}) collective-permute-start(f32[2,514,1]{1,0,2:T(2,128)S(1)} %copy.209), channel_id=1, source_target_pairs={{1,0},{2,1},{3,2},{4,3},{5,4},{6,5},{7,6},{0,7},{9,8},{10,9},{11,1... | collective-permute-start | bytes 12344 | tf_op jit(solution)/shard_map/ppermute | solution.py:19
  40.7 2.0 pad_maximum_fusion.2
  44.0 8.1 %fusion.39 = f32[2,512,512]{2,1,0:T(8,128)S(1)} fusion(f32[2,512,512]{2,1,0:T(8,128)} %copy-done.9, f32[2,514,1]{2,1,0:T(8,128)S(1)} %copy-done.16, f32[2,1,512]{2,1,0:T(1,128)S(1)} %collective-permute-done.5, f32[2,1,512]{2,1,0:T(1,128)S(1)} %collective-permute-done.4, f32[2,514,1]{2,1,0:T(8,128)} %copy-done.14, f32[2,512,514]{2,1,0:T(8,128)S(1)} %slice.600, ...), kind=kLoop, calls=%fused_computation.113 | loop fusion | flops 8912896 | bytes 6324288 | tf_op jit(solution)/shard_map/add | solution.py:45
  52.1 1.3 collective-permute-start.8
  53.3 3.0 collective-permute-start.9
  57.6 1.8 collective-permute-start.10
  59.6 3.8 %collective-permute-start.11 = (f32[2,514,1]{1,0,2:T(2,128)S(1)}, f32[2,514,1]{1,0,2:T(2,128)S(1)}, u32[]{:S(2)}, u32[]{:S(2)}) collective-permute-start(f32[2,514,1]{1,0,2:T(2,128)S(1)} %copy.215), channel_id=1, source_target_pairs={{1,0},{2,1},{3,2},{4,3},{5,4},{6,5},{7,6},{0,7},{9,8},{10,9},{11,1... | collective-permute-start | bytes 12344 | tf_op jit(solution)/shard_map/ppermute | solution.py:19
  66.1 5.0 %fusion.33 = f32[2,512,512]{2,1,0:T(8,128)S(1)} fusion(f32[2,512,512]{2,1,0:T(8,128)S(1)} %fusion.39, f32[2,514,1]{2,1,0:T(8,128)S(1)} %copy.217, f32[2,1,512]{2,1,0:T(1,128)S(1)} %collective-permute-done.9, f32[2,1,512]{2,1,0:T(1,128)S(1)} %collective-permute-done.8, f32[2,514,1]{2,1,0:T(8,128)S(1)} %copy.216, f32[2,512,514]{2,1,0:T(8,128)S(1)} %slice.603, ...), kind=kLoop, calls=%fused_computation.97 | loop fusion | flops 8912896 | bytes 6324288 | tf_op jit(solution)/shard_map/add | solution.py:45
  71.8 4.6 %collective-permute-start.13 = (f32[2,1,512]{2,1,0:T(1,128)S(1)}, f32[2,1,512]{2,1,0:T(1,128)S(1)}, u32[]{:S(2)}, u32[]{:S(2)}) collective-permute-start(f32[2,1,512]{2,1,0:T(1,128)S(1)} %get-tuple-element.85), channel_id=1, source_target_pairs={{8,0},{16,8},{24,16},{32,24},{40,32},{48,40},{56,48},{64,56},{72,6... | collective-permute-start | bytes 12296 | tf_op jit(solution)/shard_map/ppermute | solution.py:19
  77.7 2.0 collective-permute-start.14
  79.9 3.6 collective-permute-start.15
  86.0 5.0 %fusion.27 = f32[2,512,512]{2,1,0:T(8,128)S(1)} fusion(f32[2,512,512]{2,1,0:T(8,128)S(1)} %copy-done.1, f32[2,514,1]{2,1,0:T(8,128)S(1)} %copy.223, f32[2,1,512]{2,1,0:T(1,128)S(1)} %collective-permute-done.13, f32[2,1,512]{2,1,0:T(1,128)S(1)} %collective-permute-done.12, f32[2,514,1]{2,1,0:T(8,128)S(1)} %copy.222, f32[2,512,514]{2,1,0:T(8,128)S(1)} %slice.606, ...), kind=kLoop, calls=%fused_computation.81 | loop fusion | flops 8912896 | bytes 6324288 | tf_op jit(solution)/shard_map/add | solution.py:45
  91.0 5.6 %collective-permute-start.17 = (f32[2,1,512]{2,1,0:T(1,128)S(1)}, f32[2,1,512]{2,1,0:T(1,128)S(1)}, u32[]{:S(2)}, u32[]{:S(2)}) collective-permute-start(f32[2,1,512]{2,1,0:T(1,128)S(1)} %get-tuple-element.83), channel_id=1, source_target_pairs={{8,0},{16,8},{24,16},{32,24},{40,32},{48,40},{56,48},{64,56},{72,6... | collective-permute-start | bytes 12296 | tf_op jit(solution)/shard_map/ppermute | solution.py:19
  97.9 2.7 collective-permute-start.18
  100.8 2.7 collective-permute-start.19
  106.4 5.0 %fusion.21 = f32[2,512,512]{2,1,0:T(8,128)S(1)} fusion(f32[2,512,512]{2,1,0:T(8,128)S(1)} %copy-done.3, f32[2,514,1]{2,1,0:T(8,128)S(1)} %copy.229, f32[2,1,512]{2,1,0:T(1,128)S(1)} %collective-permute-done.17, f32[2,1,512]{2,1,0:T(1,128)S(1)} %collective-permute-done.16, f32[2,514,1]{2,1,0:T(8,128)S(1)} %copy.228, f32[2,512,514]{2,1,0:T(8,128)S(1)} %slice.609, ...), kind=kLoop, calls=%fused_computation.65 | loop fusion | flops 8912896 | bytes 6324288 | tf_op jit(solution)/shard_map/add | solution.py:45
  111.5 5.8 %collective-permute-start.21 = (f32[2,1,512]{2,1,0:T(1,128)S(1)}, f32[2,1,512]{2,1,0:T(1,128)S(1)}, u32[]{:S(2)}, u32[]{:S(2)}) collective-permute-start(f32[2,1,512]{2,1,0:T(1,128)S(1)} %get-tuple-element.81), channel_id=1, source_target_pairs={{8,0},{16,8},{24,16},{32,24},{40,32},{48,40},{56,48},{64,56},{72,6... | collective-permute-start | bytes 12296 | tf_op jit(solution)/shard_map/ppermute | solution.py:19
  118.6 2.3 collective-permute-start.22
  121.1 3.3 collective-permute-start.23
  127.2 5.0 %fusion.15 = f32[2,512,512]{2,1,0:T(8,128)S(1)} fusion(f32[2,512,512]{2,1,0:T(8,128)S(1)} %copy-done.5, f32[2,514,1]{2,1,0:T(8,128)S(1)} %copy.235, f32[2,1,512]{2,1,0:T(1,128)S(1)} %collective-permute-done.21, f32[2,1,512]{2,1,0:T(1,128)S(1)} %collective-permute-done.20, f32[2,514,1]{2,1,0:T(8,128)S(1)} %copy.234, f32[2,512,514]{2,1,0:T(8,128)S(1)} %slice.612, ...), kind=kLoop, calls=%fused_computation.49 | loop fusion | flops 8912896 | bytes 6324288 | tf_op jit(solution)/shard_map/add | solution.py:45
  132.3 5.8 %collective-permute-start.25 = (f32[2,1,512]{2,1,0:T(1,128)S(1)}, f32[2,1,512]{2,1,0:T(1,128)S(1)}, u32[]{:S(2)}, u32[]{:S(2)}) collective-permute-start(f32[2,1,512]{2,1,0:T(1,128)S(1)} %get-tuple-element.79), channel_id=1, source_target_pairs={{8,0},{16,8},{24,16},{32,24},{40,32},{48,40},{56,48},{64,56},{72,6... | collective-permute-start | bytes 12296 | tf_op jit(solution)/shard_map/ppermute | solution.py:19
  139.3 2.4 collective-permute-start.26
  141.9 2.8 collective-permute-start.27
  147.6 1.5 copy-done.8
  149.0 4.9 %fusion.9 = f32[2,512,512]{2,1,0:T(8,128)S(1)} fusion(f32[2,512,512]{2,1,0:T(8,128)S(1)} %copy-done.8, f32[2,514,1]{2,1,0:T(8,128)S(1)} %copy.241, f32[2,1,512]{2,1,0:T(1,128)S(1)} %collective-permute-done.25, f32[2,1,512]{2,1,0:T(1,128)S(1)} %collective-permute-done.24, f32[2,514,1]{2,1,0:T(8,128)S(1)} %copy.240, f32[2,512,514]{2,1,0:T(8,128)S(1)} %slice.615, ...), kind=kLoop, calls=%fused_computation.33 | loop fusion | flops 8912896 | bytes 6324288 | tf_op jit(solution)/shard_map/add | solution.py:45
  154.1 5.8 %collective-permute-start.29 = (f32[2,1,512]{2,1,0:T(1,128)S(1)}, f32[2,1,512]{2,1,0:T(1,128)S(1)}, u32[]{:S(2)}, u32[]{:S(2)}) collective-permute-start(f32[2,1,512]{2,1,0:T(1,128)S(1)} %get-tuple-element.77), channel_id=1, source_target_pairs={{8,0},{16,8},{24,16},{32,24},{40,32},{48,40},{56,48},{64,56},{72,6... | collective-permute-start | bytes 12296 | tf_op jit(solution)/shard_map/ppermute | solution.py:19
  161.1 2.3 collective-permute-start.30
  163.7 3.0 collective-permute-start.31
  169.6 5.9 %fusion.3 = f32[2,512,512]{2,1,0:T(8,128)} fusion(f32[2,512,512]{2,1,0:T(8,128)S(1)} %fusion.9, f32[2,514,1]{2,1,0:T(8,128)S(1)} %copy.247, f32[2,1,512]{2,1,0:T(1,128)S(1)} %collective-permute-done.29, f32[2,1,512]{2,1,0:T(1,128)S(1)} %collective-permute-done.28, f32[2,514,1]{2,1,0:T(8,128)S(1)} %copy.246, f32[2,512,514]{2,1,0:T(8,128)S(1)} %slice.618, ...), kind=kLoop, calls=%fused_computation.17 | loop fusion | flops 8912896 | bytes 6324288 | tf_op jit(solution)/shard_map/add | solution.py:45
  175.5 71.4 %reshape.326 = f32[2,128,4,128,4]{4,3,2,1,0:T(8,128)} reshape(f32[2,512,512]{2,1,0:T(8,128)} %fusion.3) | data formatting | bytes 4194304 | tf_op jit(solution)/shard_map/reshape | solution.py:104
  246.9 20.8 %reduce_sum.19 = f32[2,128,128]{2,1,0:T(8,128)S(1)} reduce(f32[2,128,4,128,4]{4,3,2,1,0:T(8,128)} %reshape.326, f32[]{:T(128)} %constant.89.clone.1), dimensions={2,4}, to_apply=%region_1.2 | reduce | flops 491520 | bytes 2228228 | tf_op jit(solution)/shard_map/reduce_sum | solution.py:104
  267.8 5.7 %collective-permute-start.33 = (f32[2,1,128]{2,1,0:T(1,128)S(1)}, f32[2,1,128]{2,1,0:T(1,128)S(1)}, u32[]{:S(2)}, u32[]{:S(2)}) collective-permute-start(f32[2,1,128]{2,1,0:T(1,128)S(1)} %get-tuple-element.113), channel_id=1, source_target_pairs={{8,0},{16,8},{24,16},{32,24},{40,32},{48,40},{56,48},{64,56},{72,6... | collective-permute-start | bytes 3080 | tf_op jit(solution)/shard_map/ppermute | solution.py:19
  274.4 4.0 %collective-permute-start.34 = (f32[2,130,1]{2,1,0:T(8,128)S(1)}, f32[2,130,1]{2,1,0:T(8,128)S(1)}, u32[]{:S(2)}, u32[]{:S(2)}) collective-permute-start(f32[2,130,1]{2,1,0:T(8,128)S(1)} %get-tuple-element.110), channel_id=1, source_target_pairs={{0,1},{1,2},{2,3},{3,4},{4,5},{5,6},{6,7},{7,0},{8,9},{9,10},{10,1... | collective-permute-start | bytes 3128 | tf_op jit(solution)/shard_map/ppermute | solution.py:17
  278.5 1.1 collective-permute-start.35
  279.6 2.4 collective-permute-done.34
  282.0 1.8 collective-permute-done.35
  286.9 18.4 %all_to_all.5 = f32[16,5,1024]{2,1,0:T(8,128)S(1)} all-to-all(f32[16,5,1024]{2,1,0:T(8,128)S(1)} %copy.251), channel_id=1, replica_groups=mesh['tile'=16,'col'=8] {'tile'}, dimensions={0} | all-to-all | bytes 655360 | tf_op jit(solution)/shard_map/all_to_all | solution.py:124
  305.8 1.3 stack.159
  307.1 1.5 convolution_bitcast_fusion
  308.6 64.7 %psum.7 = f32[16,16]{1,0:T(8,128)S(1)} all-reduce(f32[16,16]{1,0:T(8,128)S(1)} %convolution_bitcast_fusion), channel_id=1, replica_groups=mesh['tile'=16,'col'=8] {'tile','col'}, use_global_device_ids=true, to_apply=%region_2.3 | all-reduce | flops 256 | bytes 2048 | tf_op jit(solution)/shard_map/psum | solution.py:135
  (210 shorter events, 42.6 us)
Async XLA Ops:
  0.6 7.2 %copy-start.10 = (f32[512,512]{1,0:T(8,128)S(1)}, f32[512,512]{1,0:T(8,128)}, u32[]{:S(2)}) copy-start(f32[512,512]{1,0:T(8,128)} %param.5) | copy-start | bytes 3145732
  0.6 7.2 %copy-start.11 = (f32[512,512]{1,0:T(8,128)S(1)}, f32[512,512]{1,0:T(8,128)}, u32[]{:S(2)}) copy-start(f32[512,512]{1,0:T(8,128)} %param.6) | copy-start | bytes 3145732
  1.6 3.8 %collective-permute-start = (f32[2,1,512]{2,1,0:T(1,128)S(1)}, f32[2,1,512]{2,1,0:T(1,128)S(1)}, u32[]{:S(2)}, u32[]{:S(2)}) collective-permute-start(f32[2,1,512]{2,1,0:T(1,128)S(1)} %get-tuple-element.90), channel_id=1, source_target_pairs={{0,8},{8,16},{16,24},{24,32},{32,40},{40,48},{48,56},{56,64},{64,7... | collective-permute-start | bytes 12296 | tf_op jit(solution)/shard_map/ppermute | solution.py:17
  4.7 9.8 %copy-start.18 = (s32[16]{0:T(128)S(1)}, s32[16]{0:T(128)}, u32[]{:S(2)}) copy-start(s32[16]{0:T(128)} %param.9) | copy-start | bytes 196
  4.7 3.1 collective-permute-start.1
  8.2 10.1 %collective-permute-start.2 = (f32[2,514,1]{1,0,2:T(2,128)S(1)}, f32[2,514,1]{1,0,2:T(2,128)S(1)}, u32[]{:S(2)}, u32[]{:S(2)}) collective-permute-start(f32[2,514,1]{1,0,2:T(2,128)S(1)} %copy.202), channel_id=1, source_target_pairs={{0,1},{1,2},{2,3},{3,4},{4,5},{5,6},{6,7},{7,0},{8,9},{9,10},{10,1... | collective-permute-start | bytes 12344 | tf_op jit(solution)/shard_map/ppermute | solution.py:17
  12.0 6.6 %collective-permute-start.3 = (f32[2,514,1]{1,0,2:T(2,128)S(1)}, f32[2,514,1]{1,0,2:T(2,128)S(1)}, u32[]{:S(2)}, u32[]{:S(2)}) collective-permute-start(f32[2,514,1]{1,0,2:T(2,128)S(1)} %copy.203), channel_id=1, source_target_pairs={{1,0},{2,1},{3,2},{4,3},{5,4},{6,5},{7,6},{0,7},{9,8},{10,9},{11,1... | collective-permute-start | bytes 12344 | tf_op jit(solution)/shard_map/ppermute | solution.py:19
  27.8 16.1 %copy-start.9 = (f32[2,512,512]{2,1,0:T(8,128)}, f32[2,512,512]{2,1,0:T(8,128)S(1)}, u32[]{:S(2)}) copy-start(f32[2,512,512]{2,1,0:T(8,128)S(1)} %fusion.45) | copy-start | bytes 6291460
  27.8 1.6 collective-permute-start.4
  27.9 3.1 collective-permute-start.5
  33.3 6.1 %collective-permute-start.6 = (f32[2,514,1]{1,0,2:T(2,128)S(1)}, f32[2,514,1]{1,0,2:T(2,128)S(1)}, u32[]{:S(2)}, u32[]{:S(2)}) collective-permute-start(f32[2,514,1]{1,0,2:T(2,128)S(1)} %copy.208), channel_id=1, source_target_pairs={{0,1},{1,2},{2,3},{3,4},{4,5},{5,6},{6,7},{7,0},{8,9},{9,10},{10,1... | collective-permute-start | bytes 12344 | tf_op jit(solution)/shard_map/ppermute | solution.py:17
  34.3 5.4 %collective-permute-start.7 = (f32[2,514,1]{1,0,2:T(2,128)S(1)}, f32[2,514,1]{1,0,2:T(2,128)S(1)}, u32[]{:S(2)}, u32[]{:S(2)}) collective-permute-start(f32[2,514,1]{1,0,2:T(2,128)S(1)} %copy.209), channel_id=1, source_target_pairs={{1,0},{2,1},{3,2},{4,3},{5,4},{6,5},{7,6},{0,7},{9,8},{10,9},{11,1... | collective-permute-start | bytes 12344 | tf_op jit(solution)/shard_map/ppermute | solution.py:19
  52.1 4.9 %collective-permute-start.8 = (f32[2,1,512]{2,1,0:T(1,128)S(1)}, f32[2,1,512]{2,1,0:T(1,128)S(1)}, u32[]{:S(2)}, u32[]{:S(2)}) collective-permute-start(f32[2,1,512]{2,1,0:T(1,128)S(1)} %get-tuple-element.86), channel_id=1, source_target_pairs={{0,8},{8,16},{16,24},{24,32},{32,40},{40,48},{48,56},{56,64},{64,7... | collective-permute-start | bytes 12296 | tf_op jit(solution)/shard_map/ppermute | solution.py:17
  53.3 3.8 %collective-permute-start.9 = (f32[2,1,512]{2,1,0:T(1,128)S(1)}, f32[2,1,512]{2,1,0:T(1,128)S(1)}, u32[]{:S(2)}, u32[]{:S(2)}) collective-permute-start(f32[2,1,512]{2,1,0:T(1,128)S(1)} %get-tuple-element.87), channel_id=1, source_target_pairs={{8,0},{16,8},{24,16},{32,24},{40,32},{48,40},{56,48},{64,56},{72,6... | collective-permute-start | bytes 12296 | tf_op jit(solution)/shard_map/ppermute | solution.py:19
  57.6 6.6 %collective-permute-start.10 = (f32[2,514,1]{1,0,2:T(2,128)S(1)}, f32[2,514,1]{1,0,2:T(2,128)S(1)}, u32[]{:S(2)}, u32[]{:S(2)}) collective-permute-start(f32[2,514,1]{1,0,2:T(2,128)S(1)} %copy.214), channel_id=1, source_target_pairs={{0,1},{1,2},{2,3},{3,4},{4,5},{5,6},{6,7},{7,0},{8,9},{9,10},{10,1... | collective-permute-start | bytes 12344 | tf_op jit(solution)/shard_map/ppermute | solution.py:17
  59.6 4.8 %collective-permute-start.11 = (f32[2,514,1]{1,0,2:T(2,128)S(1)}, f32[2,514,1]{1,0,2:T(2,128)S(1)}, u32[]{:S(2)}, u32[]{:S(2)}) collective-permute-start(f32[2,514,1]{1,0,2:T(2,128)S(1)} %copy.215), channel_id=1, source_target_pairs={{1,0},{2,1},{3,2},{4,3},{5,4},{6,5},{7,6},{0,7},{9,8},{10,9},{11,1... | collective-permute-start | bytes 12344 | tf_op jit(solution)/shard_map/ppermute | solution.py:19
  71.1 5.9 %collective-permute-start.12 = (f32[2,1,512]{2,1,0:T(1,128)S(1)}, f32[2,1,512]{2,1,0:T(1,128)S(1)}, u32[]{:S(2)}, u32[]{:S(2)}) collective-permute-start(f32[2,1,512]{2,1,0:T(1,128)S(1)} %get-tuple-element.84), channel_id=1, source_target_pairs={{0,8},{8,16},{16,24},{24,32},{32,40},{40,48},{48,56},{56,64},{64,7... | collective-permute-start | bytes 12296 | tf_op jit(solution)/shard_map/ppermute | solution.py:17
  71.8 5.4 %collective-permute-start.13 = (f32[2,1,512]{2,1,0:T(1,128)S(1)}, f32[2,1,512]{2,1,0:T(1,128)S(1)}, u32[]{:S(2)}, u32[]{:S(2)}) collective-permute-start(f32[2,1,512]{2,1,0:T(1,128)S(1)} %get-tuple-element.85), channel_id=1, source_target_pairs={{8,0},{16,8},{24,16},{32,24},{40,32},{48,40},{56,48},{64,56},{72,6... | collective-permute-start | bytes 12296 | tf_op jit(solution)/shard_map/ppermute | solution.py:19
  77.5 7.1 %copy-start.1 = (f32[2,512,512]{2,1,0:T(8,128)S(1)}, f32[2,512,512]{2,1,0:T(8,128)}, u32[]{:S(2)}) copy-start(f32[2,512,512]{2,1,0:T(8,128)} %copy-done) | copy-start | bytes 6291460
  77.7 6.4 %collective-permute-start.14 = (f32[2,514,1]{1,0,2:T(2,128)S(1)}, f32[2,514,1]{1,0,2:T(2,128)S(1)}, u32[]{:S(2)}, u32[]{:S(2)}) collective-permute-start(f32[2,514,1]{1,0,2:T(2,128)S(1)} %copy.220), channel_id=1, source_target_pairs={{0,1},{1,2},{2,3},{3,4},{4,5},{5,6},{6,7},{7,0},{8,9},{9,10},{10,1... | collective-permute-start | bytes 12344 | tf_op jit(solution)/shard_map/ppermute | solution.py:17
  79.9 4.4 %collective-permute-start.15 = (f32[2,514,1]{1,0,2:T(2,128)S(1)}, f32[2,514,1]{1,0,2:T(2,128)S(1)}, u32[]{:S(2)}, u32[]{:S(2)}) collective-permute-start(f32[2,514,1]{1,0,2:T(2,128)S(1)} %copy.221), channel_id=1, source_target_pairs={{1,0},{2,1},{3,2},{4,3},{5,4},{6,5},{7,6},{0,7},{9,8},{10,9},{11,1... | collective-permute-start | bytes 12344 | tf_op jit(solution)/shard_map/ppermute | solution.py:19
  90.9 6.3 %collective-permute-start.16 = (f32[2,1,512]{2,1,0:T(1,128)S(1)}, f32[2,1,512]{2,1,0:T(1,128)S(1)}, u32[]{:S(2)}, u32[]{:S(2)}) collective-permute-start(f32[2,1,512]{2,1,0:T(1,128)S(1)} %get-tuple-element.82), channel_id=1, source_target_pairs={{0,8},{8,16},{16,24},{24,32},{32,40},{40,48},{48,56},{56,64},{64,7... | collective-permute-start | bytes 12296 | tf_op jit(solution)/shard_map/ppermute | solution.py:17
  91.0 6.4 %collective-permute-start.17 = (f32[2,1,512]{2,1,0:T(1,128)S(1)}, f32[2,1,512]{2,1,0:T(1,128)S(1)}, u32[]{:S(2)}, u32[]{:S(2)}) collective-permute-start(f32[2,1,512]{2,1,0:T(1,128)S(1)} %get-tuple-element.83), channel_id=1, source_target_pairs={{8,0},{16,8},{24,16},{32,24},{40,32},{48,40},{56,48},{64,56},{72,6... | collective-permute-start | bytes 12296 | tf_op jit(solution)/shard_map/ppermute | solution.py:19
  97.7 7.3 %copy-start.3 = (f32[2,512,512]{2,1,0:T(8,128)S(1)}, f32[2,512,512]{2,1,0:T(8,128)}, u32[]{:S(2)}) copy-start(f32[2,512,512]{2,1,0:T(8,128)} %copy-done.2) | copy-start | bytes 6291460
  97.9 6.3 %collective-permute-start.18 = (f32[2,514,1]{1,0,2:T(2,128)S(1)}, f32[2,514,1]{1,0,2:T(2,128)S(1)}, u32[]{:S(2)}, u32[]{:S(2)}) collective-permute-start(f32[2,514,1]{1,0,2:T(2,128)S(1)} %copy.226), channel_id=1, source_target_pairs={{0,1},{1,2},{2,3},{3,4},{4,5},{5,6},{6,7},{7,0},{8,9},{9,10},{10,1... | collective-permute-start | bytes 12344 | tf_op jit(solution)/shard_map/ppermute | solution.py:17
  100.8 4.0 %collective-permute-start.19 = (f32[2,514,1]{1,0,2:T(2,128)S(1)}, f32[2,514,1]{1,0,2:T(2,128)S(1)}, u32[]{:S(2)}, u32[]{:S(2)}) collective-permute-start(f32[2,514,1]{1,0,2:T(2,128)S(1)} %copy.227), channel_id=1, source_target_pairs={{1,0},{2,1},{3,2},{4,3},{5,4},{6,5},{7,6},{0,7},{9,8},{10,9},{11,1... | collective-permute-start | bytes 12344 | tf_op jit(solution)/shard_map/ppermute | solution.py:19
  111.4 6.7 %copy-start.4 = (f32[2,512,512]{2,1,0:T(8,128)}, f32[2,512,512]{2,1,0:T(8,128)S(1)}, u32[]{:S(2)}) copy-start(f32[2,512,512]{2,1,0:T(8,128)S(1)} %fusion.21) | copy-start | bytes 6291460
  111.4 6.4 %collective-permute-start.20 = (f32[2,1,512]{2,1,0:T(1,128)S(1)}, f32[2,1,512]{2,1,0:T(1,128)S(1)}, u32[]{:S(2)}, u32[]{:S(2)}) collective-permute-start(f32[2,1,512]{2,1,0:T(1,128)S(1)} %get-tuple-element.80), channel_id=1, source_target_pairs={{0,8},{8,16},{16,24},{24,32},{32,40},{40,48},{48,56},{56,64},{64,7... | collective-permute-start | bytes 12296 | tf_op jit(solution)/shard_map/ppermute | solution.py:17
  111.5 6.6 %collective-permute-start.21 = (f32[2,1,512]{2,1,0:T(1,128)S(1)}, f32[2,1,512]{2,1,0:T(1,128)S(1)}, u32[]{:S(2)}, u32[]{:S(2)}) collective-permute-start(f32[2,1,512]{2,1,0:T(1,128)S(1)} %get-tuple-element.81), channel_id=1, source_target_pairs={{8,0},{16,8},{24,16},{32,24},{40,32},{48,40},{56,48},{64,56},{72,6... | collective-permute-start | bytes 12296 | tf_op jit(solution)/shard_map/ppermute | solution.py:19
  118.3 7.5 %copy-start.5 = (f32[2,512,512]{2,1,0:T(8,128)S(1)}, f32[2,512,512]{2,1,0:T(8,128)}, u32[]{:S(2)}) copy-start(f32[2,512,512]{2,1,0:T(8,128)} %copy-done.4) | copy-start | bytes 6291460
  118.6 6.1 %collective-permute-start.22 = (f32[2,514,1]{1,0,2:T(2,128)S(1)}, f32[2,514,1]{1,0,2:T(2,128)S(1)}, u32[]{:S(2)}, u32[]{:S(2)}) collective-permute-start(f32[2,514,1]{1,0,2:T(2,128)S(1)} %copy.232), channel_id=1, source_target_pairs={{0,1},{1,2},{2,3},{3,4},{4,5},{5,6},{6,7},{7,0},{8,9},{9,10},{10,1... | collective-permute-start | bytes 12344 | tf_op jit(solution)/shard_map/ppermute | solution.py:17
  121.1 4.5 %collective-permute-start.23 = (f32[2,514,1]{1,0,2:T(2,128)S(1)}, f32[2,514,1]{1,0,2:T(2,128)S(1)}, u32[]{:S(2)}, u32[]{:S(2)}) collective-permute-start(f32[2,514,1]{1,0,2:T(2,128)S(1)} %copy.233), channel_id=1, source_target_pairs={{1,0},{2,1},{3,2},{4,3},{5,4},{6,5},{7,6},{0,7},{9,8},{10,9},{11,1... | collective-permute-start | bytes 12344 | tf_op jit(solution)/shard_map/ppermute | solution.py:19
  132.2 6.4 %collective-permute-start.24 = (f32[2,1,512]{2,1,0:T(1,128)S(1)}, f32[2,1,512]{2,1,0:T(1,128)S(1)}, u32[]{:S(2)}, u32[]{:S(2)}) collective-permute-start(f32[2,1,512]{2,1,0:T(1,128)S(1)} %get-tuple-element.78), channel_id=1, source_target_pairs={{0,8},{8,16},{16,24},{24,32},{32,40},{40,48},{48,56},{56,64},{64,7... | collective-permute-start | bytes 12296 | tf_op jit(solution)/shard_map/ppermute | solution.py:17
  132.3 6.6 %collective-permute-start.25 = (f32[2,1,512]{2,1,0:T(1,128)S(1)}, f32[2,1,512]{2,1,0:T(1,128)S(1)}, u32[]{:S(2)}, u32[]{:S(2)}) collective-permute-start(f32[2,1,512]{2,1,0:T(1,128)S(1)} %get-tuple-element.79), channel_id=1, source_target_pairs={{8,0},{16,8},{24,16},{32,24},{40,32},{48,40},{56,48},{64,56},{72,6... | collective-permute-start | bytes 12296 | tf_op jit(solution)/shard_map/ppermute | solution.py:19
  139.1 7.1 %copy-start.7 = (f32[2,512,512]{2,1,0:T(8,128)S(1)}, f32[2,512,512]{2,1,0:T(8,128)}, u32[]{:S(2)}) copy-start(f32[2,512,512]{2,1,0:T(8,128)} %copy-done.6) | copy-start | bytes 6291460
  139.3 6.1 %collective-permute-start.26 = (f32[2,514,1]{1,0,2:T(2,128)S(1)}, f32[2,514,1]{1,0,2:T(2,128)S(1)}, u32[]{:S(2)}, u32[]{:S(2)}) collective-permute-start(f32[2,514,1]{1,0,2:T(2,128)S(1)} %copy.238), channel_id=1, source_target_pairs={{0,1},{1,2},{2,3},{3,4},{4,5},{5,6},{6,7},{7,0},{8,9},{9,10},{10,1... | collective-permute-start | bytes 12344 | tf_op jit(solution)/shard_map/ppermute | solution.py:17
  141.9 4.0 %collective-permute-start.27 = (f32[2,514,1]{1,0,2:T(2,128)S(1)}, f32[2,514,1]{1,0,2:T(2,128)S(1)}, u32[]{:S(2)}, u32[]{:S(2)}) collective-permute-start(f32[2,514,1]{1,0,2:T(2,128)S(1)} %copy.239), channel_id=1, source_target_pairs={{1,0},{2,1},{3,2},{4,3},{5,4},{6,5},{7,6},{0,7},{9,8},{10,9},{11,1... | collective-permute-start | bytes 12344 | tf_op jit(solution)/shard_map/ppermute | solution.py:19
  154.0 6.4 %collective-permute-start.28 = (f32[2,1,512]{2,1,0:T(1,128)S(1)}, f32[2,1,512]{2,1,0:T(1,128)S(1)}, u32[]{:S(2)}, u32[]{:S(2)}) collective-permute-start(f32[2,1,512]{2,1,0:T(1,128)S(1)} %get-tuple-element.76), channel_id=1, source_target_pairs={{0,8},{8,16},{16,24},{24,32},{32,40},{40,48},{48,56},{56,64},{64,7... | collective-permute-start | bytes 12296 | tf_op jit(solution)/shard_map/ppermute | solution.py:17
  154.1 12.6 %copy-start.19 = (s32[4,4]{1,0:T(4,128)S(1)}, s32[4,4]{1,0:T(4,128)}, u32[]{:S(2)}) copy-start(s32[4,4]{1,0:T(4,128)} %param.7) | copy-start | bytes 196
  154.1 12.7 %copy-start.20 = (s32[4,4]{1,0:T(4,128)S(1)}, s32[4,4]{1,0:T(4,128)}, u32[]{:S(2)}) copy-start(s32[4,4]{1,0:T(4,128)} %param.8) | copy-start | bytes 196
  154.1 6.6 %collective-permute-start.29 = (f32[2,1,512]{2,1,0:T(1,128)S(1)}, f32[2,1,512]{2,1,0:T(1,128)S(1)}, u32[]{:S(2)}, u32[]{:S(2)}) collective-permute-start(f32[2,1,512]{2,1,0:T(1,128)S(1)} %get-tuple-element.77), channel_id=1, source_target_pairs={{8,0},{16,8},{24,16},{32,24},{40,32},{48,40},{56,48},{64,56},{72,6... | collective-permute-start | bytes 12296 | tf_op jit(solution)/shard_map/ppermute | solution.py:19
  161.1 6.1 %collective-permute-start.30 = (f32[2,514,1]{1,0,2:T(2,128)S(1)}, f32[2,514,1]{1,0,2:T(2,128)S(1)}, u32[]{:S(2)}, u32[]{:S(2)}) collective-permute-start(f32[2,514,1]{1,0,2:T(2,128)S(1)} %copy.244), channel_id=1, source_target_pairs={{0,1},{1,2},{2,3},{3,4},{4,5},{5,6},{6,7},{7,0},{8,9},{9,10},{10,1... | collective-permute-start | bytes 12344 | tf_op jit(solution)/shard_map/ppermute | solution.py:17
  163.7 4.3 %collective-permute-start.31 = (f32[2,514,1]{1,0,2:T(2,128)S(1)}, f32[2,514,1]{1,0,2:T(2,128)S(1)}, u32[]{:S(2)}, u32[]{:S(2)}) collective-permute-start(f32[2,514,1]{1,0,2:T(2,128)S(1)} %copy.245), channel_id=1, source_target_pairs={{1,0},{2,1},{3,2},{4,3},{5,4},{6,5},{7,6},{0,7},{9,8},{10,9},{11,1... | collective-permute-start | bytes 12344 | tf_op jit(solution)/shard_map/ppermute | solution.py:19
  267.7 6.3 %collective-permute-start.32 = (f32[2,1,128]{2,1,0:T(1,128)S(1)}, f32[2,1,128]{2,1,0:T(1,128)S(1)}, u32[]{:S(2)}, u32[]{:S(2)}) collective-permute-start(f32[2,1,128]{2,1,0:T(1,128)S(1)} %get-tuple-element.112), channel_id=1, source_target_pairs={{0,8},{8,16},{16,24},{24,32},{32,40},{40,48},{48,56},{56,64},{64,7... | collective-permute-start | bytes 3080 | tf_op jit(solution)/shard_map/ppermute | solution.py:17
  267.8 6.5 %collective-permute-start.33 = (f32[2,1,128]{2,1,0:T(1,128)S(1)}, f32[2,1,128]{2,1,0:T(1,128)S(1)}, u32[]{:S(2)}, u32[]{:S(2)}) collective-permute-start(f32[2,1,128]{2,1,0:T(1,128)S(1)} %get-tuple-element.113), channel_id=1, source_target_pairs={{8,0},{16,8},{24,16},{32,24},{40,32},{48,40},{56,48},{64,56},{72,6... | collective-permute-start | bytes 3080 | tf_op jit(solution)/shard_map/ppermute | solution.py:19
  274.4 7.6 %collective-permute-start.34 = (f32[2,130,1]{2,1,0:T(8,128)S(1)}, f32[2,130,1]{2,1,0:T(8,128)S(1)}, u32[]{:S(2)}, u32[]{:S(2)}) collective-permute-start(f32[2,130,1]{2,1,0:T(8,128)S(1)} %get-tuple-element.110), channel_id=1, source_target_pairs={{0,1},{1,2},{2,3},{3,4},{4,5},{5,6},{6,7},{7,0},{8,9},{9,10},{10,1... | collective-permute-start | bytes 3128 | tf_op jit(solution)/shard_map/ppermute | solution.py:17
  278.5 5.4 %collective-permute-start.35 = (f32[2,130,1]{2,1,0:T(8,128)S(1)}, f32[2,130,1]{2,1,0:T(8,128)S(1)}, u32[]{:S(2)}, u32[]{:S(2)}) collective-permute-start(f32[2,130,1]{2,1,0:T(8,128)S(1)} %get-tuple-element.111), channel_id=1, source_target_pairs={{1,0},{2,1},{3,2},{4,3},{5,4},{6,5},{7,6},{0,7},{9,8},{10,9},{11,1... | collective-permute-start | bytes 3128 | tf_op jit(solution)/shard_map/ppermute | solution.py:19
  307.1 66.8 %copy-start.17 = (f32[16,16,1024]{2,1,0:T(8,128)}, f32[16,16,1024]{2,1,0:T(8,128)S(1)}, u32[]{:S(2)}) copy-start(f32[16,16,1024]{2,1,0:T(8,128)S(1)} %stack.159) | copy-start | bytes 3145732
  (9 other events, 30.4 us)
where the time goes:
time: 381 us; the launch traced here: 374 us
  starting transfers between devices  91.9 us (24%)
  local copies, waits for them, and re-layouts  89.5 us (23%)
  blocking collectives  83.1 us (22%)
  other arithmetic  81.8 us (21%)
  waiting for transfers between devices  20.8 us (5%)
  between operations  5.18 us (1%)
    reshape x1, local copies, waits for them, and re-layouts, per_device(): field.reshape(2, fine_rows // 4, 4, fine_cols // 4, 4).mean(axis=(2, 4))  71.4 us
    psum x1, blocking collectives, per_device(): gram = lax.psum(part, ('tile', 'col')) / (fine_rows // 4 * (fine_cols // 4))  64.7 us
    ppermute x18, starting transfers between devices, with_halo(): lax.ppermute(head, axis, [((i + 1) % count, i) for i in range(count)])  64.6 us
    add x8, other arithmetic, relax(): return centre + KAPPA * (beside_all - 4.0 * centre)  45.1 us
    ppermute x18, starting transfers between devices, with_halo(): lax.ppermute(tail, axis, [(i, (i + 1) % count) for i in range(count)])  27.3 us
    reduce_sum x1, other arithmetic, per_device(): field.reshape(2, fine_rows // 4, 4, fine_cols // 4, 4).mean(axis=(2, 4))  20.8 us
    all_to_all x1, blocking collectives, per_device(): lax.all_to_all(jnp.einsum('vh,hsd->vsd', chosen_terms, starting_tile_set,...  18.4 us
    ppermute x18, waiting for transfers between devices, with_halo(): lax.ppermute(tail, axis, [(i, (i + 1) % count) for i in range(count)])  11.6 us
  transfers between devices with their start and end apart: 36, of which 31 were waited for; matrix products, arithmetic and copies ran while one was open for 1% of the time, Pallas kernels for 0%

commit v1 on v0

--- a/solution.py
+++ b/solution.py
@@ -132,7 +132,7 @@
         )
     )
     part = jnp.einsum("pnc,pmc->nm", library, library, precision=lax.Precision.HIGHEST)
-    gram = lax.psum(part, ("tile", "col")) / (fine_rows // 4 * (fine_cols // 4))
+    gram = lax.psum(lax.psum(part, "col"), "tile") / (fine_rows // 4 * (fine_cols // 4))
     return (library[None, None], gram)
 
 

time: 381 us -> 368 us (0.966)
  blocking collectives: 83.1 us -> 70.4 us
    psum x1 -> x2, blocking collectives: 64.7 us -> 52 us  [the longest x1 32 us: per_device(): lax.psum(lax.psum(part, 'col'), 'tile')]
where the time goes in v1:
time: 368 us; the launch traced here: 361 us
  starting transfers between devices  91.8 us (25%)
  local copies, waits for them, and re-layouts  89.5 us (24%)
  other arithmetic  81.8 us (22%)
  blocking collectives  70.4 us (19%)
  waiting for transfers between devices  20.8 us (6%)
  between operations  5.21 us (1%)
    reshape x1, local copies, waits for them, and re-layouts, per_device(): field.reshape(2, fine_rows // 4, 4, fine_cols // 4, 4).mean(axis=(2, 4))  71.4 us
    ppermute x18, starting transfers between devices, with_halo(): lax.ppermute(head, axis, [((i + 1) % count, i) for i in range(count)])  64.6 us
    add x8, other arithmetic, relax(): return centre + KAPPA * (beside_all - 4.0 * centre)  45.1 us
    psum x1, blocking collectives, per_device(): lax.psum(lax.psum(part, 'col'), 'tile')  32 us
    ppermute x18, starting transfers between devices, with_halo(): lax.ppermute(tail, axis, [(i, (i + 1) % count) for i in range(count)])  27.3 us
    reduce_sum x1, other arithmetic, per_device(): field.reshape(2, fine_rows // 4, 4, fine_cols // 4, 4).mean(axis=(2, 4))  20.8 us
    psum x1, blocking collectives, per_device(): lax.psum(part, 'col')  20 us
    all_to_all x1, blocking collectives, per_device(): lax.all_to_all(jnp.einsum('vh,hsd->vsd', chosen_terms, starting_tile_set,...  18.4 us
  transfers between devices with their start and end apart: 36, of which 31 were waited for; matrix products, arithmetic and copies ran while one was open for 1% of the time, Pallas kernels for 0%

profile of v1, /device:TPU:1, one launch (start us, length us, event | category | flops | bytes accessed | tf_op | source)
XLA Modules:
  0.0 361.3 jit_solution(17026217738489612826)
XLA Ops:
  1.6 3.1 collective-permute-start
  5.4 2.4 collective-permute-done.1
  8.2 3.5 collective-permute-start.2
  12.0 2.5 collective-permute-start.3
  21.4 6.4 %fusion.45 = f32[2,512,512]{2,1,0:T(8,128)S(1)} fusion(f32[2,514,1]{2,1,0:T(8,128)} %copy-done.15, f32[2,1,512]{2,1,0:T(1,128)S(1)} %collective-permute-done.1, f32[2,1,512]{2,1,0:T(1,128)S(1)} %collective-permute-done, f32[1,512,512]{2,1,0:T(8,128)S(1)} %bitcast.34, f32[1,512,512]{2,1,0:T(8,128)S(1)} %bitcast.28, f32[2,514,1]{2,1,0:T(8,128)} %copy-done.13, ...), kind=kLoop, calls=%fused_computation.129 | loop fusion | flops 10485760 | bytes 6324288 | tf_op jit(solution)/shard_map/add | solution.py:45
  29.4 1.5 collective-permute-done.5
  32.0 1.3 copy.208
  34.3 4.6 %collective-permute-start.7 = (f32[2,514,1]{1,0,2:T(2,128)S(1)}, f32[2,514,1]{1,0,2:T(2,128)S(1)}, u32[]{:S(2)}, u32[]{:S(2)}) collective-permute-start(f32[2,514,1]{1,0,2:T(2,128)S(1)} %copy.209), channel_id=1, source_target_pairs={{1,0},{2,1},{3,2},{4,3},{5,4},{6,5},{7,6},{0,7},{9,8},{10,9},{11,1... | collective-permute-start | bytes 12344 | tf_op jit(solution)/shard_map/ppermute | solution.py:19
  40.7 2.0 pad_maximum_fusion.2
  44.0 8.1 %fusion.39 = f32[2,512,512]{2,1,0:T(8,128)S(1)} fusion(f32[2,512,512]{2,1,0:T(8,128)} %copy-done.9, f32[2,514,1]{2,1,0:T(8,128)S(1)} %copy-done.16, f32[2,1,512]{2,1,0:T(1,128)S(1)} %collective-permute-done.5, f32[2,1,512]{2,1,0:T(1,128)S(1)} %collective-permute-done.4, f32[2,514,1]{2,1,0:T(8,128)} %copy-done.14, f32[2,512,514]{2,1,0:T(8,128)S(1)} %slice.600, ...), kind=kLoop, calls=%fused_computation.113 | loop fusion | flops 8912896 | bytes 6324288 | tf_op jit(solution)/shard_map/add | solution.py:45
  52.1 1.3 collective-permute-start.8
  53.3 3.0 collective-permute-start.9
  57.6 1.8 collective-permute-start.10
  59.6 3.8 %collective-permute-start.11 = (f32[2,514,1]{1,0,2:T(2,128)S(1)}, f32[2,514,1]{1,0,2:T(2,128)S(1)}, u32[]{:S(2)}, u32[]{:S(2)}) collective-permute-start(f32[2,514,1]{1,0,2:T(2,128)S(1)} %copy.215), channel_id=1, source_target_pairs={{1,0},{2,1},{3,2},{4,3},{5,4},{6,5},{7,6},{0,7},{9,8},{10,9},{11,1... | collective-permute-start | bytes 12344 | tf_op jit(solution)/shard_map/ppermute | solution.py:19
  66.1 5.0 %fusion.33 = f32[2,512,512]{2,1,0:T(8,128)S(1)} fusion(f32[2,512,512]{2,1,0:T(8,128)S(1)} %fusion.39, f32[2,514,1]{2,1,0:T(8,128)S(1)} %copy.217, f32[2,1,512]{2,1,0:T(1,128)S(1)} %collective-permute-done.9, f32[2,1,512]{2,1,0:T(1,128)S(1)} %collective-permute-done.8, f32[2,514,1]{2,1,0:T(8,128)S(1)} %copy.216, f32[2,512,514]{2,1,0:T(8,128)S(1)} %slice.603, ...), kind=kLoop, calls=%fused_computation.97 | loop fusion | flops 8912896 | bytes 6324288 | tf_op jit(solution)/shard_map/add | solution.py:45
  71.8 4.6 %collective-permute-start.13 = (f32[2,1,512]{2,1,0:T(1,128)S(1)}, f32[2,1,512]{2,1,0:T(1,128)S(1)}, u32[]{:S(2)}, u32[]{:S(2)}) collective-permute-start(f32[2,1,512]{2,1,0:T(1,128)S(1)} %get-tuple-element.85), channel_id=1, source_target_pairs={{8,0},{16,8},{24,16},{32,24},{40,32},{48,40},{56,48},{64,56},{72,6... | collective-permute-start | bytes 12296 | tf_op jit(solution)/shard_map/ppermute | solution.py:19
  77.7 2.0 collective-permute-start.14
  79.9 3.6 %collective-permute-start.15 = (f32[2,514,1]{1,0,2:T(2,128)S(1)}, f32[2,514,1]{1,0,2:T(2,128)S(1)}, u32[]{:S(2)}, u32[]{:S(2)}) collective-permute-start(f32[2,514,1]{1,0,2:T(2,128)S(1)} %copy.221), channel_id=1, source_target_pairs={{1,0},{2,1},{3,2},{4,3},{5,4},{6,5},{7,6},{0,7},{9,8},{10,9},{11,1... | collective-permute-start | bytes 12344 | tf_op jit(solution)/shard_map/ppermute | solution.py:19
  86.0 5.0 %fusion.27 = f32[2,512,512]{2,1,0:T(8,128)S(1)} fusion(f32[2,512,512]{2,1,0:T(8,128)S(1)} %copy-done.1, f32[2,514,1]{2,1,0:T(8,128)S(1)} %copy.223, f32[2,1,512]{2,1,0:T(1,128)S(1)} %collective-permute-done.13, f32[2,1,512]{2,1,0:T(1,128)S(1)} %collective-permute-done.12, f32[2,514,1]{2,1,0:T(8,128)S(1)} %copy.222, f32[2,512,514]{2,1,0:T(8,128)S(1)} %slice.606, ...), kind=kLoop, calls=%fused_computation.81 | loop fusion | flops 8912896 | bytes 6324288 | tf_op jit(solution)/shard_map/add | solution.py:45
  91.0 5.6 %collective-permute-start.17 = (f32[2,1,512]{2,1,0:T(1,128)S(1)}, f32[2,1,512]{2,1,0:T(1,128)S(1)}, u32[]{:S(2)}, u32[]{:S(2)}) collective-permute-start(f32[2,1,512]{2,1,0:T(1,128)S(1)} %get-tuple-element.83), channel_id=1, source_target_pairs={{8,0},{16,8},{24,16},{32,24},{40,32},{48,40},{56,48},{64,56},{72,6... | collective-permute-start | bytes 12296 | tf_op jit(solution)/shard_map/ppermute | solution.py:19
  97.9 2.7 collective-permute-start.18
  100.8 2.7 collective-permute-start.19
  106.4 5.0 %fusion.21 = f32[2,512,512]{2,1,0:T(8,128)S(1)} fusion(f32[2,512,512]{2,1,0:T(8,128)S(1)} %copy-done.3, f32[2,514,1]{2,1,0:T(8,128)S(1)} %copy.229, f32[2,1,512]{2,1,0:T(1,128)S(1)} %collective-permute-done.17, f32[2,1,512]{2,1,0:T(1,128)S(1)} %collective-permute-done.16, f32[2,514,1]{2,1,0:T(8,128)S(1)} %copy.228, f32[2,512,514]{2,1,0:T(8,128)S(1)} %slice.609, ...), kind=kLoop, calls=%fused_computation.65 | loop fusion | flops 8912896 | bytes 6324288 | tf_op jit(solution)/shard_map/add | solution.py:45
  111.5 5.8 %collective-permute-start.21 = (f32[2,1,512]{2,1,0:T(1,128)S(1)}, f32[2,1,512]{2,1,0:T(1,128)S(1)}, u32[]{:S(2)}, u32[]{:S(2)}) collective-permute-start(f32[2,1,512]{2,1,0:T(1,128)S(1)} %get-tuple-element.81), channel_id=1, source_target_pairs={{8,0},{16,8},{24,16},{32,24},{40,32},{48,40},{56,48},{64,56},{72,6... | collective-permute-start | bytes 12296 | tf_op jit(solution)/shard_map/ppermute | solution.py:19
  118.6 2.3 collective-permute-start.22
  121.1 3.3 collective-permute-start.23
  127.1 5.0 %fusion.15 = f32[2,512,512]{2,1,0:T(8,128)S(1)} fusion(f32[2,512,512]{2,1,0:T(8,128)S(1)} %copy-done.5, f32[2,514,1]{2,1,0:T(8,128)S(1)} %copy.235, f32[2,1,512]{2,1,0:T(1,128)S(1)} %collective-permute-done.21, f32[2,1,512]{2,1,0:T(1,128)S(1)} %collective-permute-done.20, f32[2,514,1]{2,1,0:T(8,128)S(1)} %copy.234, f32[2,512,514]{2,1,0:T(8,128)S(1)} %slice.612, ...), kind=kLoop, calls=%fused_computation.49 | loop fusion | flops 8912896 | bytes 6324288 | tf_op jit(solution)/shard_map/add | solution.py:45
  132.2 5.8 %collective-permute-start.25 = (f32[2,1,512]{2,1,0:T(1,128)S(1)}, f32[2,1,512]{2,1,0:T(1,128)S(1)}, u32[]{:S(2)}, u32[]{:S(2)}) collective-permute-start(f32[2,1,512]{2,1,0:T(1,128)S(1)} %get-tuple-element.79), channel_id=1, source_target_pairs={{8,0},{16,8},{24,16},{32,24},{40,32},{48,40},{56,48},{64,56},{72,6... | collective-permute-start | bytes 12296 | tf_op jit(solution)/shard_map/ppermute | solution.py:19
  139.3 2.4 collective-permute-start.26
  141.9 2.8 collective-permute-start.27
  147.5 1.5 copy-done.8
  149.0 4.9 %fusion.9 = f32[2,512,512]{2,1,0:T(8,128)S(1)} fusion(f32[2,512,512]{2,1,0:T(8,128)S(1)} %copy-done.8, f32[2,514,1]{2,1,0:T(8,128)S(1)} %copy.241, f32[2,1,512]{2,1,0:T(1,128)S(1)} %collective-permute-done.25, f32[2,1,512]{2,1,0:T(1,128)S(1)} %collective-permute-done.24, f32[2,514,1]{2,1,0:T(8,128)S(1)} %copy.240, f32[2,512,514]{2,1,0:T(8,128)S(1)} %slice.615, ...), kind=kLoop, calls=%fused_computation.33 | loop fusion | flops 8912896 | bytes 6324288 | tf_op jit(solution)/shard_map/add | solution.py:45
  154.0 5.8 %collective-permute-start.29 = (f32[2,1,512]{2,1,0:T(1,128)S(1)}, f32[2,1,512]{2,1,0:T(1,128)S(1)}, u32[]{:S(2)}, u32[]{:S(2)}) collective-permute-start(f32[2,1,512]{2,1,0:T(1,128)S(1)} %get-tuple-element.77), channel_id=1, source_target_pairs={{8,0},{16,8},{24,16},{32,24},{40,32},{48,40},{56,48},{64,56},{72,6... | collective-permute-start | bytes 12296 | tf_op jit(solution)/shard_map/ppermute | solution.py:19
  161.1 2.3 collective-permute-start.30
  163.6 3.0 collective-permute-start.31
  169.5 5.9 %fusion.3 = f32[2,512,512]{2,1,0:T(8,128)} fusion(f32[2,512,512]{2,1,0:T(8,128)S(1)} %fusion.9, f32[2,514,1]{2,1,0:T(8,128)S(1)} %copy.247, f32[2,1,512]{2,1,0:T(1,128)S(1)} %collective-permute-done.29, f32[2,1,512]{2,1,0:T(1,128)S(1)} %collective-permute-done.28, f32[2,514,1]{2,1,0:T(8,128)S(1)} %copy.246, f32[2,512,514]{2,1,0:T(8,128)S(1)} %slice.618, ...), kind=kLoop, calls=%fused_computation.17 | loop fusion | flops 8912896 | bytes 6324288 | tf_op jit(solution)/shard_map/add | solution.py:45
  175.4 71.4 %reshape.326 = f32[2,128,4,128,4]{4,3,2,1,0:T(8,128)} reshape(f32[2,512,512]{2,1,0:T(8,128)} %fusion.3) | data formatting | bytes 4194304 | tf_op jit(solution)/shard_map/reshape | solution.py:104
  246.9 20.8 %reduce_sum.19 = f32[2,128,128]{2,1,0:T(8,128)S(1)} reduce(f32[2,128,4,128,4]{4,3,2,1,0:T(8,128)} %reshape.326, f32[]{:T(128)} %constant.89.clone.1), dimensions={2,4}, to_apply=%region_1.2 | reduce | flops 491520 | bytes 2228228 | tf_op jit(solution)/shard_map/reduce_sum | solution.py:104
  267.7 5.7 %collective-permute-start.33 = (f32[2,1,128]{2,1,0:T(1,128)S(1)}, f32[2,1,128]{2,1,0:T(1,128)S(1)}, u32[]{:S(2)}, u32[]{:S(2)}) collective-permute-start(f32[2,1,128]{2,1,0:T(1,128)S(1)} %get-tuple-element.113), channel_id=1, source_target_pairs={{8,0},{16,8},{24,16},{32,24},{40,32},{48,40},{56,48},{64,56},{72,6... | collective-permute-start | bytes 3080 | tf_op jit(solution)/shard_map/ppermute | solution.py:19
  274.4 4.0 %collective-permute-start.34 = (f32[2,130,1]{2,1,0:T(8,128)S(1)}, f32[2,130,1]{2,1,0:T(8,128)S(1)}, u32[]{:S(2)}, u32[]{:S(2)}) collective-permute-start(f32[2,130,1]{2,1,0:T(8,128)S(1)} %get-tuple-element.110), channel_id=1, source_target_pairs={{0,1},{1,2},{2,3},{3,4},{4,5},{5,6},{6,7},{7,0},{8,9},{9,10},{10,1... | collective-permute-start | bytes 3128 | tf_op jit(solution)/shard_map/ppermute | solution.py:17
  278.4 1.1 collective-permute-start.35
  279.5 2.4 collective-permute-done.34
  281.9 1.8 collective-permute-done.35
  286.8 18.4 %all_to_all.5 = f32[16,5,1024]{2,1,0:T(8,128)S(1)} all-to-all(f32[16,5,1024]{2,1,0:T(8,128)S(1)} %copy.251), channel_id=1, replica_groups=mesh['tile'=16,'col'=8] {'tile'}, dimensions={0} | all-to-all | bytes 655360 | tf_op jit(solution)/shard_map/all_to_all | solution.py:124
  305.7 1.3 stack.159
  307.0 1.5 convolution_bitcast_fusion
  308.5 20.0 %psum.14 = f32[16,16]{1,0:T(8,128)S(1)} all-reduce(f32[16,16]{1,0:T(8,128)S(1)} %convolution_bitcast_fusion), channel_id=1, replica_groups=mesh['tile'=16,'col'=8] {'col'}, use_global_device_ids=true, to_apply=%region_2.3 | all-reduce | flops 256 | bytes 2048 | tf_op jit(solution)/shard_map/psum | solution.py:135
  328.5 32.0 %psum.15 = f32[16,16]{1,0:T(8,128)S(1)} all-reduce(f32[16,16]{1,0:T(8,128)S(1)} %psum.14), channel_id=1, replica_groups=mesh['tile'=16,'col'=8] {'tile'}, use_global_device_ids=true, to_apply=%region_3.4 | all-reduce | flops 256 | bytes 2048 | tf_op jit(solution)/shard_map/psum | solution.py:135
  (211 shorter events, 43.7 us)
Async XLA Ops:
  0.6 7.2 %copy-start.10 = (f32[512,512]{1,0:T(8,128)S(1)}, f32[512,512]{1,0:T(8,128)}, u32[]{:S(2)}) copy-start(f32[512,512]{1,0:T(8,128)} %param.5) | copy-start | bytes 3145732
  0.6 7.2 %copy-start.11 = (f32[512,512]{1,0:T(8,128)S(1)}, f32[512,512]{1,0:T(8,128)}, u32[]{:S(2)}) copy-start(f32[512,512]{1,0:T(8,128)} %param.6) | copy-start | bytes 3145732
  1.6 3.8 %collective-permute-start = (f32[2,1,512]{2,1,0:T(1,128)S(1)}, f32[2,1,512]{2,1,0:T(1,128)S(1)}, u32[]{:S(2)}, u32[]{:S(2)}) collective-permute-start(f32[2,1,512]{2,1,0:T(1,128)S(1)} %get-tuple-element.90), channel_id=1, source_target_pairs={{0,8},{8,16},{16,24},{24,32},{32,40},{40,48},{48,56},{56,64},{64,7... | collective-permute-start | bytes 12296 | tf_op jit(solution)/shard_map/ppermute | solution.py:17
  4.7 9.8 %copy-start.18 = (s32[16]{0:T(128)S(1)}, s32[16]{0:T(128)}, u32[]{:S(2)}) copy-start(s32[16]{0:T(128)} %param.9) | copy-start | bytes 196
  4.7 3.1 collective-permute-start.1
  8.2 10.1 %collective-permute-start.2 = (f32[2,514,1]{1,0,2:T(2,128)S(1)}, f32[2,514,1]{1,0,2:T(2,128)S(1)}, u32[]{:S(2)}, u32[]{:S(2)}) collective-permute-start(f32[2,514,1]{1,0,2:T(2,128)S(1)} %copy.202), channel_id=1, source_target_pairs={{0,1},{1,2},{2,3},{3,4},{4,5},{5,6},{6,7},{7,0},{8,9},{9,10},{10,1... | collective-permute-start | bytes 12344 | tf_op jit(solution)/shard_map/ppermute | solution.py:17
  12.0 6.6 %collective-permute-start.3 = (f32[2,514,1]{1,0,2:T(2,128)S(1)}, f32[2,514,1]{1,0,2:T(2,128)S(1)}, u32[]{:S(2)}, u32[]{:S(2)}) collective-permute-start(f32[2,514,1]{1,0,2:T(2,128)S(1)} %copy.203), channel_id=1, source_target_pairs={{1,0},{2,1},{3,2},{4,3},{5,4},{6,5},{7,6},{0,7},{9,8},{10,9},{11,1... | collective-permute-start | bytes 12344 | tf_op jit(solution)/shard_map/ppermute | solution.py:19
  27.8 16.1 %copy-start.9 = (f32[2,512,512]{2,1,0:T(8,128)}, f32[2,512,512]{2,1,0:T(8,128)S(1)}, u32[]{:S(2)}) copy-start(f32[2,512,512]{2,1,0:T(8,128)S(1)} %fusion.45) | copy-start | bytes 6291460
  27.8 1.6 collective-permute-start.4
  27.9 3.1 collective-permute-start.5
  33.3 6.1 %collective-permute-start.6 = (f32[2,514,1]{1,0,2:T(2,128)S(1)}, f32[2,514,1]{1,0,2:T(2,128)S(1)}, u32[]{:S(2)}, u32[]{:S(2)}) collective-permute-start(f32[2,514,1]{1,0,2:T(2,128)S(1)} %copy.208), channel_id=1, source_target_pairs={{0,1},{1,2},{2,3},{3,4},{4,5},{5,6},{6,7},{7,0},{8,9},{9,10},{10,1... | collective-permute-start | bytes 12344 | tf_op jit(solution)/shard_map/ppermute | solution.py:17
  34.3 5.4 %collective-permute-start.7 = (f32[2,514,1]{1,0,2:T(2,128)S(1)}, f32[2,514,1]{1,0,2:T(2,128)S(1)}, u32[]{:S(2)}, u32[]{:S(2)}) collective-permute-start(f32[2,514,1]{1,0,2:T(2,128)S(1)} %copy.209), channel_id=1, source_target_pairs={{1,0},{2,1},{3,2},{4,3},{5,4},{6,5},{7,6},{0,7},{9,8},{10,9},{11,1... | collective-permute-start | bytes 12344 | tf_op jit(solution)/shard_map/ppermute | solution.py:19
  52.1 4.9 %collective-permute-start.8 = (f32[2,1,512]{2,1,0:T(1,128)S(1)}, f32[2,1,512]{2,1,0:T(1,128)S(1)}, u32[]{:S(2)}, u32[]{:S(2)}) collective-permute-start(f32[2,1,512]{2,1,0:T(1,128)S(1)} %get-tuple-element.86), channel_id=1, source_target_pairs={{0,8},{8,16},{16,24},{24,32},{32,40},{40,48},{48,56},{56,64},{64,7... | collective-permute-start | bytes 12296 | tf_op jit(solution)/shard_map/ppermute | solution.py:17
  53.3 3.8 %collective-permute-start.9 = (f32[2,1,512]{2,1,0:T(1,128)S(1)}, f32[2,1,512]{2,1,0:T(1,128)S(1)}, u32[]{:S(2)}, u32[]{:S(2)}) collective-permute-start(f32[2,1,512]{2,1,0:T(1,128)S(1)} %get-tuple-element.87), channel_id=1, source_target_pairs={{8,0},{16,8},{24,16},{32,24},{40,32},{48,40},{56,48},{64,56},{72,6... | collective-permute-start | bytes 12296 | tf_op jit(solution)/shard_map/ppermute | solution.py:19
  57.6 6.6 %collective-permute-start.10 = (f32[2,514,1]{1,0,2:T(2,128)S(1)}, f32[2,514,1]{1,0,2:T(2,128)S(1)}, u32[]{:S(2)}, u32[]{:S(2)}) collective-permute-start(f32[2,514,1]{1,0,2:T(2,128)S(1)} %copy.214), channel_id=1, source_target_pairs={{0,1},{1,2},{2,3},{3,4},{4,5},{5,6},{6,7},{7,0},{8,9},{9,10},{10,1... | collective-permute-start | bytes 12344 | tf_op jit(solution)/shard_map/ppermute | solution.py:17
  59.6 4.8 %collective-permute-start.11 = (f32[2,514,1]{1,0,2:T(2,128)S(1)}, f32[2,514,1]{1,0,2:T(2,128)S(1)}, u32[]{:S(2)}, u32[]{:S(2)}) collective-permute-start(f32[2,514,1]{1,0,2:T(2,128)S(1)} %copy.215), channel_id=1, source_target_pairs={{1,0},{2,1},{3,2},{4,3},{5,4},{6,5},{7,6},{0,7},{9,8},{10,9},{11,1... | collective-permute-start | bytes 12344 | tf_op jit(solution)/shard_map/ppermute | solution.py:19
  71.1 5.9 %collective-permute-start.12 = (f32[2,1,512]{2,1,0:T(1,128)S(1)}, f32[2,1,512]{2,1,0:T(1,128)S(1)}, u32[]{:S(2)}, u32[]{:S(2)}) collective-permute-start(f32[2,1,512]{2,1,0:T(1,128)S(1)} %get-tuple-element.84), channel_id=1, source_target_pairs={{0,8},{8,16},{16,24},{24,32},{32,40},{40,48},{48,56},{56,64},{64,7... | collective-permute-start | bytes 12296 | tf_op jit(solution)/shard_map/ppermute | solution.py:17
  71.8 5.4 %collective-permute-start.13 = (f32[2,1,512]{2,1,0:T(1,128)S(1)}, f32[2,1,512]{2,1,0:T(1,128)S(1)}, u32[]{:S(2)}, u32[]{:S(2)}) collective-permute-start(f32[2,1,512]{2,1,0:T(1,128)S(1)} %get-tuple-element.85), channel_id=1, source_target_pairs={{8,0},{16,8},{24,16},{32,24},{40,32},{48,40},{56,48},{64,56},{72,6... | collective-permute-start | bytes 12296 | tf_op jit(solution)/shard_map/ppermute | solution.py:19
  77.5 7.1 %copy-start.1 = (f32[2,512,512]{2,1,0:T(8,128)S(1)}, f32[2,512,512]{2,1,0:T(8,128)}, u32[]{:S(2)}) copy-start(f32[2,512,512]{2,1,0:T(8,128)} %copy-done) | copy-start | bytes 6291460
  77.7 6.4 %collective-permute-start.14 = (f32[2,514,1]{1,0,2:T(2,128)S(1)}, f32[2,514,1]{1,0,2:T(2,128)S(1)}, u32[]{:S(2)}, u32[]{:S(2)}) collective-permute-start(f32[2,514,1]{1,0,2:T(2,128)S(1)} %copy.220), channel_id=1, source_target_pairs={{0,1},{1,2},{2,3},{3,4},{4,5},{5,6},{6,7},{7,0},{8,9},{9,10},{10,1... | collective-permute-start | bytes 12344 | tf_op jit(solution)/shard_map/ppermute | solution.py:17
  79.9 4.4 %collective-permute-start.15 = (f32[2,514,1]{1,0,2:T(2,128)S(1)}, f32[2,514,1]{1,0,2:T(2,128)S(1)}, u32[]{:S(2)}, u32[]{:S(2)}) collective-permute-start(f32[2,514,1]{1,0,2:T(2,128)S(1)} %copy.221), channel_id=1, source_target_pairs={{1,0},{2,1},{3,2},{4,3},{5,4},{6,5},{7,6},{0,7},{9,8},{10,9},{11,1... | collective-permute-start | bytes 12344 | tf_op jit(solution)/shard_map/ppermute | solution.py:19
  91.0 6.3 %collective-permute-start.16 = (f32[2,1,512]{2,1,0:T(1,128)S(1)}, f32[2,1,512]{2,1,0:T(1,128)S(1)}, u32[]{:S(2)}, u32[]{:S(2)}) collective-permute-start(f32[2,1,512]{2,1,0:T(1,128)S(1)} %get-tuple-element.82), channel_id=1, source_target_pairs={{0,8},{8,16},{16,24},{24,32},{32,40},{40,48},{48,56},{56,64},{64,7... | collective-permute-start | bytes 12296 | tf_op jit(solution)/shard_map/ppermute | solution.py:17
  91.0 6.4 %collective-permute-start.17 = (f32[2,1,512]{2,1,0:T(1,128)S(1)}, f32[2,1,512]{2,1,0:T(1,128)S(1)}, u32[]{:S(2)}, u32[]{:S(2)}) collective-permute-start(f32[2,1,512]{2,1,0:T(1,128)S(1)} %get-tuple-element.83), channel_id=1, source_target_pairs={{8,0},{16,8},{24,16},{32,24},{40,32},{48,40},{56,48},{64,56},{72,6... | collective-permute-start | bytes 12296 | tf_op jit(solution)/shard_map/ppermute | solution.py:19
  97.7 7.3 %copy-start.3 = (f32[2,512,512]{2,1,0:T(8,128)S(1)}, f32[2,512,512]{2,1,0:T(8,128)}, u32[]{:S(2)}) copy-start(f32[2,512,512]{2,1,0:T(8,128)} %copy-done.2) | copy-start | bytes 6291460
  97.9 6.3 %collective-permute-start.18 = (f32[2,514,1]{1,0,2:T(2,128)S(1)}, f32[2,514,1]{1,0,2:T(2,128)S(1)}, u32[]{:S(2)}, u32[]{:S(2)}) collective-permute-start(f32[2,514,1]{1,0,2:T(2,128)S(1)} %copy.226), channel_id=1, source_target_pairs={{0,1},{1,2},{2,3},{3,4},{4,5},{5,6},{6,7},{7,0},{8,9},{9,10},{10,1... | collective-permute-start | bytes 12344 | tf_op jit(solution)/shard_map/ppermute | solution.py:17
  100.8 4.0 %collective-permute-start.19 = (f32[2,514,1]{1,0,2:T(2,128)S(1)}, f32[2,514,1]{1,0,2:T(2,128)S(1)}, u32[]{:S(2)}, u32[]{:S(2)}) collective-permute-start(f32[2,514,1]{1,0,2:T(2,128)S(1)} %copy.227), channel_id=1, source_target_pairs={{1,0},{2,1},{3,2},{4,3},{5,4},{6,5},{7,6},{0,7},{9,8},{10,9},{11,1... | collective-permute-start | bytes 12344 | tf_op jit(solution)/shard_map/ppermute | solution.py:19
  111.4 6.7 %copy-start.4 = (f32[2,512,512]{2,1,0:T(8,128)}, f32[2,512,512]{2,1,0:T(8,128)S(1)}, u32[]{:S(2)}) copy-start(f32[2,512,512]{2,1,0:T(8,128)S(1)} %fusion.21) | copy-start | bytes 6291460
  111.4 6.4 %collective-permute-start.20 = (f32[2,1,512]{2,1,0:T(1,128)S(1)}, f32[2,1,512]{2,1,0:T(1,128)S(1)}, u32[]{:S(2)}, u32[]{:S(2)}) collective-permute-start(f32[2,1,512]{2,1,0:T(1,128)S(1)} %get-tuple-element.80), channel_id=1, source_target_pairs={{0,8},{8,16},{16,24},{24,32},{32,40},{40,48},{48,56},{56,64},{64,7... | collective-permute-start | bytes 12296 | tf_op jit(solution)/shard_map/ppermute | solution.py:17
  111.5 6.6 %collective-permute-start.21 = (f32[2,1,512]{2,1,0:T(1,128)S(1)}, f32[2,1,512]{2,1,0:T(1,128)S(1)}, u32[]{:S(2)}, u32[]{:S(2)}) collective-permute-start(f32[2,1,512]{2,1,0:T(1,128)S(1)} %get-tuple-element.81), channel_id=1, source_target_pairs={{8,0},{16,8},{24,16},{32,24},{40,32},{48,40},{56,48},{64,56},{72,6... | collective-permute-start | bytes 12296 | tf_op jit(solution)/shard_map/ppermute | solution.py:19
  118.3 7.4 %copy-start.5 = (f32[2,512,512]{2,1,0:T(8,128)S(1)}, f32[2,512,512]{2,1,0:T(8,128)}, u32[]{:S(2)}) copy-start(f32[2,512,512]{2,1,0:T(8,128)} %copy-done.4) | copy-start | bytes 6291460
  118.6 6.1 %collective-permute-start.22 = (f32[2,514,1]{1,0,2:T(2,128)S(1)}, f32[2,514,1]{1,0,2:T(2,128)S(1)}, u32[]{:S(2)}, u32[]{:S(2)}) collective-permute-start(f32[2,514,1]{1,0,2:T(2,128)S(1)} %copy.232), channel_id=1, source_target_pairs={{0,1},{1,2},{2,3},{3,4},{4,5},{5,6},{6,7},{7,0},{8,9},{9,10},{10,1... | collective-permute-start | bytes 12344 | tf_op jit(solution)/shard_map/ppermute | solution.py:17
  121.1 4.4 %collective-permute-start.23 = (f32[2,514,1]{1,0,2:T(2,128)S(1)}, f32[2,514,1]{1,0,2:T(2,128)S(1)}, u32[]{:S(2)}, u32[]{:S(2)}) collective-permute-start(f32[2,514,1]{1,0,2:T(2,128)S(1)} %copy.233), channel_id=1, source_target_pairs={{1,0},{2,1},{3,2},{4,3},{5,4},{6,5},{7,6},{0,7},{9,8},{10,9},{11,1... | collective-permute-start | bytes 12344 | tf_op jit(solution)/shard_map/ppermute | solution.py:19
  132.1 6.4 %collective-permute-start.24 = (f32[2,1,512]{2,1,0:T(1,128)S(1)}, f32[2,1,512]{2,1,0:T(1,128)S(1)}, u32[]{:S(2)}, u32[]{:S(2)}) collective-permute-start(f32[2,1,512]{2,1,0:T(1,128)S(1)} %get-tuple-element.78), channel_id=1, source_target_pairs={{0,8},{8,16},{16,24},{24,32},{32,40},{40,48},{48,56},{56,64},{64,7... | collective-permute-start | bytes 12296 | tf_op jit(solution)/shard_map/ppermute | solution.py:17
  132.2 6.6 %collective-permute-start.25 = (f32[2,1,512]{2,1,0:T(1,128)S(1)}, f32[2,1,512]{2,1,0:T(1,128)S(1)}, u32[]{:S(2)}, u32[]{:S(2)}) collective-permute-start(f32[2,1,512]{2,1,0:T(1,128)S(1)} %get-tuple-element.79), channel_id=1, source_target_pairs={{8,0},{16,8},{24,16},{32,24},{40,32},{48,40},{56,48},{64,56},{72,6... | collective-permute-start | bytes 12296 | tf_op jit(solution)/shard_map/ppermute | solution.py:19
  139.0 7.1 %copy-start.7 = (f32[2,512,512]{2,1,0:T(8,128)S(1)}, f32[2,512,512]{2,1,0:T(8,128)}, u32[]{:S(2)}) copy-start(f32[2,512,512]{2,1,0:T(8,128)} %copy-done.6) | copy-start | bytes 6291460
  139.3 6.1 %collective-permute-start.26 = (f32[2,514,1]{1,0,2:T(2,128)S(1)}, f32[2,514,1]{1,0,2:T(2,128)S(1)}, u32[]{:S(2)}, u32[]{:S(2)}) collective-permute-start(f32[2,514,1]{1,0,2:T(2,128)S(1)} %copy.238), channel_id=1, source_target_pairs={{0,1},{1,2},{2,3},{3,4},{4,5},{5,6},{6,7},{7,0},{8,9},{9,10},{10,1... | collective-permute-start | bytes 12344 | tf_op jit(solution)/shard_map/ppermute | solution.py:17
  141.9 4.0 %collective-permute-start.27 = (f32[2,514,1]{1,0,2:T(2,128)S(1)}, f32[2,514,1]{1,0,2:T(2,128)S(1)}, u32[]{:S(2)}, u32[]{:S(2)}) collective-permute-start(f32[2,514,1]{1,0,2:T(2,128)S(1)} %copy.239), channel_id=1, source_target_pairs={{1,0},{2,1},{3,2},{4,3},{5,4},{6,5},{7,6},{0,7},{9,8},{10,9},{11,1... | collective-permute-start | bytes 12344 | tf_op jit(solution)/shard_map/ppermute | solution.py:19
  153.9 6.4 %collective-permute-start.28 = (f32[2,1,512]{2,1,0:T(1,128)S(1)}, f32[2,1,512]{2,1,0:T(1,128)S(1)}, u32[]{:S(2)}, u32[]{:S(2)}) collective-permute-start(f32[2,1,512]{2,1,0:T(1,128)S(1)} %get-tuple-element.76), channel_id=1, source_target_pairs={{0,8},{8,16},{16,24},{24,32},{32,40},{40,48},{48,56},{56,64},{64,7... | collective-permute-start | bytes 12296 | tf_op jit(solution)/shard_map/ppermute | solution.py:17
  154.0 12.6 %copy-start.19 = (s32[4,4]{1,0:T(4,128)S(1)}, s32[4,4]{1,0:T(4,128)}, u32[]{:S(2)}) copy-start(s32[4,4]{1,0:T(4,128)} %param.7) | copy-start | bytes 196
  154.0 12.7 %copy-start.20 = (s32[4,4]{1,0:T(4,128)S(1)}, s32[4,4]{1,0:T(4,128)}, u32[]{:S(2)}) copy-start(s32[4,4]{1,0:T(4,128)} %param.8) | copy-start | bytes 196
  154.0 6.6 %collective-permute-start.29 = (f32[2,1,512]{2,1,0:T(1,128)S(1)}, f32[2,1,512]{2,1,0:T(1,128)S(1)}, u32[]{:S(2)}, u32[]{:S(2)}) collective-permute-start(f32[2,1,512]{2,1,0:T(1,128)S(1)} %get-tuple-element.77), channel_id=1, source_target_pairs={{8,0},{16,8},{24,16},{32,24},{40,32},{48,40},{56,48},{64,56},{72,6... | collective-permute-start | bytes 12296 | tf_op jit(solution)/shard_map/ppermute | solution.py:19
  161.1 6.1 %collective-permute-start.30 = (f32[2,514,1]{1,0,2:T(2,128)S(1)}, f32[2,514,1]{1,0,2:T(2,128)S(1)}, u32[]{:S(2)}, u32[]{:S(2)}) collective-permute-start(f32[2,514,1]{1,0,2:T(2,128)S(1)} %copy.244), channel_id=1, source_target_pairs={{0,1},{1,2},{2,3},{3,4},{4,5},{5,6},{6,7},{7,0},{8,9},{9,10},{10,1... | collective-permute-start | bytes 12344 | tf_op jit(solution)/shard_map/ppermute | solution.py:17
  163.6 4.3 %collective-permute-start.31 = (f32[2,514,1]{1,0,2:T(2,128)S(1)}, f32[2,514,1]{1,0,2:T(2,128)S(1)}, u32[]{:S(2)}, u32[]{:S(2)}) collective-permute-start(f32[2,514,1]{1,0,2:T(2,128)S(1)} %copy.245), channel_id=1, source_target_pairs={{1,0},{2,1},{3,2},{4,3},{5,4},{6,5},{7,6},{0,7},{9,8},{10,9},{11,1... | collective-permute-start | bytes 12344 | tf_op jit(solution)/shard_map/ppermute | solution.py:19
  267.7 6.3 %collective-permute-start.32 = (f32[2,1,128]{2,1,0:T(1,128)S(1)}, f32[2,1,128]{2,1,0:T(1,128)S(1)}, u32[]{:S(2)}, u32[]{:S(2)}) collective-permute-start(f32[2,1,128]{2,1,0:T(1,128)S(1)} %get-tuple-element.112), channel_id=1, source_target_pairs={{0,8},{8,16},{16,24},{24,32},{32,40},{40,48},{48,56},{56,64},{64,7... | collective-permute-start | bytes 3080 | tf_op jit(solution)/shard_map/ppermute | solution.py:17
  267.7 6.5 %collective-permute-start.33 = (f32[2,1,128]{2,1,0:T(1,128)S(1)}, f32[2,1,128]{2,1,0:T(1,128)S(1)}, u32[]{:S(2)}, u32[]{:S(2)}) collective-permute-start(f32[2,1,128]{2,1,0:T(1,128)S(1)} %get-tuple-element.113), channel_id=1, source_target_pairs={{8,0},{16,8},{24,16},{32,24},{40,32},{48,40},{56,48},{64,56},{72,6... | collective-permute-start | bytes 3080 | tf_op jit(solution)/shard_map/ppermute | solution.py:19
  274.4 7.6 %collective-permute-start.34 = (f32[2,130,1]{2,1,0:T(8,128)S(1)}, f32[2,130,1]{2,1,0:T(8,128)S(1)}, u32[]{:S(2)}, u32[]{:S(2)}) collective-permute-start(f32[2,130,1]{2,1,0:T(8,128)S(1)} %get-tuple-element.110), channel_id=1, source_target_pairs={{0,1},{1,2},{2,3},{3,4},{4,5},{5,6},{6,7},{7,0},{8,9},{9,10},{10,1... | collective-permute-start | bytes 3128 | tf_op jit(solution)/shard_map/ppermute | solution.py:17
  278.4 5.4 %collective-permute-start.35 = (f32[2,130,1]{2,1,0:T(8,128)S(1)}, f32[2,130,1]{2,1,0:T(8,128)S(1)}, u32[]{:S(2)}, u32[]{:S(2)}) collective-permute-start(f32[2,130,1]{2,1,0:T(8,128)S(1)} %get-tuple-element.111), channel_id=1, source_target_pairs={{1,0},{2,1},{3,2},{4,3},{5,4},{6,5},{7,6},{0,7},{9,8},{10,9},{11,1... | collective-permute-start | bytes 3128 | tf_op jit(solution)/shard_map/ppermute | solution.py:19
  307.0 54.1 %copy-start.17 = (f32[16,16,1024]{2,1,0:T(8,128)}, f32[16,16,1024]{2,1,0:T(8,128)S(1)}, u32[]{:S(2)}) copy-start(f32[16,16,1024]{2,1,0:T(8,128)S(1)} %stack.159) | copy-start | bytes 3145732
  (9 other events, 30.4 us)
